TPU v7x, 256 devices: a whole 4x4x8 slice. The times are simulated.
256 devices in a mesh: dp: 4 (over z_lo, core), seq: 64 (over y, x, z_hi).
Axes of the slice: x: 4, y: 4, z: 8 (z_hi: 4, z_lo: 2; z = z_hi * 2 + z_lo), core: 2. Of those that a mesh axis runs over, the one named last changes fastest.
Arguments:
- traces_in: bfloat16 [8, 512, 512, 128], P('dp', 'seq'), may hold values from -6 to 6
- w_value: bfloat16 [128, 128], replicated, may hold values from -0.5 to 0.5
- w_gate: bfloat16 [128, 128], replicated, may hold values from -0.5 to 0.5
- first_blocks: bfloat16 [512, 512, 512], P('seq', 'dp'), may hold values from -0.25 to 0.25
- second_blocks: bfloat16 [512, 512, 512], P('seq', 'dp'), may hold values from -0.25 to 0.25
- cotangent: bfloat16 [8, 512, 512, 128], P('dp', 'seq'), may hold values from -6 to 6
Outputs:
- mixed: bfloat16 [8, 512, 512, 128], P('dp', 'seq')
- grad_in: bfloat16 [8, 512, 512, 128], P('dp', 'seq')
- grad_first: bfloat16 [512, 512, 512], P('seq', 'dp')
- grad_second: bfloat16 [512, 512, 512], P('seq', 'dp')
All inputs are finite; a program needn't handle non-finite values.
Results may differ from a plain program's by a relative error of at most 0.015.
Values may be sent and summed in bfloat16 or wider, within the bound.
A program may use at most 128 MiB of HBM per device.

v0:
```python
import jax
import jax.numpy as jnp
from jax import lax
from jax.sharding import PartitionSpec as P


def on_device(traces_in, w_value, w_gate, first_blocks, second_blocks, cotangent):
    full_first, full_second = (
        lax.all_gather(first_blocks, "dp", axis=1, tiled=True),
        lax.all_gather(second_blocks, "dp", axis=1, tiled=True),
    )
    values = jnp.einsum(
        "tpqc,cd->tpqd", traces_in, w_value, preferred_element_type=jnp.float32
    ).astype(jnp.bfloat16)
    gates = jnp.einsum("tpqc,cd->tpqd", traces_in, w_gate, preferred_element_type=jnp.float32)
    sig = jax.nn.sigmoid(gates)
    act = gates * sig
    rowmix = jnp.einsum(
        "pij,tpjc->tpic", full_first, values, preferred_element_type=jnp.float32
    ).astype(jnp.bfloat16)
    gradf = cotangent.astype(jnp.float32)
    d_col = (gradf * act).astype(jnp.bfloat16)
    columns = lax.all_to_all(rowmix, "seq", split_axis=2, concat_axis=1, tiled=True)
    mixed_cols = jnp.einsum(
        "qij,tjqc->tiqc", full_second, columns, preferred_element_type=jnp.float32
    )
    colmix_cols = mixed_cols.astype(jnp.bfloat16)
    colmix = lax.all_to_all(colmix_cols, "seq", split_axis=1, concat_axis=2, tiled=True)
    cotan_cols = lax.all_to_all(d_col, "seq", split_axis=2, concat_axis=1, tiled=True)
    back = jnp.einsum("qij,tiqc->tjqc", full_second, cotan_cols, preferred_element_type=jnp.float32)
    d_row_cols = back.astype(jnp.bfloat16)
    d_row = lax.all_to_all(d_row_cols, "seq", split_axis=1, concat_axis=2, tiled=True)
    colf = colmix.astype(jnp.float32)
    mixed = (colf * act).astype(jnp.bfloat16)
    d_gate = (gradf * colf * sig * (1.0 + gates * (1.0 - sig))).astype(jnp.bfloat16)
    d_val = jnp.einsum(
        "pij,tpic->tpjc", full_first, d_row, preferred_element_type=jnp.float32
    ).astype(jnp.bfloat16)
    grad_in = jnp.einsum("tpqd,cd->tpqc", d_val, w_value, preferred_element_type=jnp.float32)
    grad_in = (
        grad_in + jnp.einsum("tpqd,cd->tpqc", d_gate, w_gate, preferred_element_type=jnp.float32)
    ).astype(jnp.bfloat16)
    trace_count = traces_in.shape[0] * lax.axis_size("dp")
    second_part = jnp.einsum(
        "tiqc,tjqc->qij", cotan_cols, columns, preferred_element_type=jnp.float32
    )
    second_sum = lax.psum_scatter(
        second_part.astype(jnp.bfloat16), "dp", scatter_dimension=1, tiled=True
    ).astype(jnp.float32)
    first_part = jnp.einsum("tpic,tpjc->pij", d_row, values, preferred_element_type=jnp.float32)
    first_sum = lax.psum_scatter(
        first_part.astype(jnp.bfloat16), "dp", scatter_dimension=1, tiled=True
    ).astype(jnp.float32)
    grad_first = (first_sum / trace_count).astype(jnp.bfloat16)
    grad_second = (second_sum / trace_count).astype(jnp.bfloat16)
    return (mixed, grad_in, grad_first, grad_second)


def solution(mesh):
    return jax.shard_map(
        on_device,
        mesh=mesh,
        in_specs=(
            P("dp", "seq", None, None),
            P(),
            P(),
            P("seq", "dp", None),
            P("seq", "dp", None),
            P("dp", "seq", None, None),
        ),
        out_specs=(
            P("dp", "seq", None, None),
            P("dp", "seq", None, None),
            P("seq", "dp", None),
            P("seq", "dp", None),
        ),
        check_vma=False,
    )
```

profile of v0, /device:TPU:1, one launch (start us, length us, event | category | flops | bytes accessed | tf_op | source)
XLA Modules:
  0.0 446.5 jit_solution(18387896903272516224)
XLA Ops:
  7.2 0.0 copy-start
  7.2 0.0 copy-start.7
  7.2 0.0 all-gather.3.cloned.1.call-start
  7.2 0.7 all-gather.3.cloned.1.call-update
  7.9 0.0 all-gather.5.cloned.1.call-start
  8.0 0.7 all-gather.5.cloned.1.call-update
  8.7 0.0 reduce-scatter.5.cloned.1.call-start
  8.7 0.0 copy-done
  8.8 0.0 copy-done.7
  8.8 2.0 convolution_convert_fusion
  10.8 52.5 %all-gather.3.cloned.1.call-done = bf16[8,512,512]{2,1,0:T(8,128)(2,1)} async-done(((bf16[8,128,512]{2,1,0:T(8,128)(2,1)}), bf16[8,512,512]{2,1,0:T(8,128)(2,1)}) %all-gather.3.cloned.1.call-update) | async-done | bytes 4194320 | tf_op jit(solution)/shard_map/all_gather | solution.py:9
  63.3 5.5 %convert_bitcast_fusion.3 = bf16[2,8,512,128]{2,3,0,1:T(8,128)(2,1)} fusion(bf16[8,512,512]{2,1,0:T(8,128)(2,1)} %all-gather.3.cloned.1.call-done, bf16[2,8,512,128]{3,2,1,0:T(8,128)(2,1)} %convolution_convert_fusion), kind=kOutput, calls=%fused_computation.33 | convolution fusion | flops 1074790400 | bytes 8388608 | tf_op jit(solution)/shard_map/pij,tpjc->tpic/dot_general | solution.py:18
  68.7 6.2 %copy.50 = bf16[2,8,512,128]{3,0,1,2:T(2,128)(2,1)} copy(bf16[2,8,512,128]{2,3,0,1:T(8,128)(2,1)} %convert_bitcast_fusion.3) | data formatting | bytes 4194304 | tf_op jit(solution)/shard_map/convert_element_type | solution.py:20
  74.9 88.4 %all_to_all.63 = bf16[2,8,512,128]{3,0,1,2:T(2,128)(2,1)S(1)} all-to-all(bf16[2,8,512,128]{3,0,1,2:T(2,128)(2,1)} %copy.50), channel_id=1, replica_groups=mesh['dp'=4,'seq'=64] {'seq'}, dimensions={2} | all-to-all | bytes 4194304 | tf_op jit(solution)/shard_map/all_to_all | solution.py:23
  163.3 0.5 copy.103
  163.9 2.0 copy.52
  165.8 5.6 %convert_bitcast_fusion.2 = bf16[2,512,8,128]{1,3,0,2:T(8,128)(2,1)} fusion(bf16[8,512,512]{2,1,0:T(8,128)(2,1)} %all-gather.5.cloned.1.call-done, bf16[2,512,8,128]{3,2,1,0:T(8,128)(2,1)} %bitcast.92), kind=kOutput, calls=%fused_computation.32 | convolution fusion | flops 1074790400 | bytes 8388608 | tf_op jit(solution)/shard_map/qij,tjqc->tiqc/dot_general | solution.py:24
  171.4 6.2 %copy.54 = bf16[2,512,8,128]{3,0,2,1:T(2,128)(2,1)} copy(bf16[2,512,8,128]{1,3,0,2:T(8,128)(2,1)} %convert_bitcast_fusion.2) | data formatting | bytes 4194304 | tf_op jit(solution)/shard_map/convert_element_type | solution.py:27
  177.6 50.9 %all_to_all.64 = bf16[2,512,8,128]{3,0,2,1:T(2,128)(2,1)S(1)} all-to-all(bf16[2,512,8,128]{3,0,2,1:T(2,128)(2,1)} %copy.54), channel_id=1, replica_groups=mesh['dp'=4,'seq'=64] {'seq'}, dimensions={1} | all-to-all | bytes 4194304 | tf_op jit(solution)/shard_map/all_to_all | solution.py:28
  228.5 0.3 copy.55
  228.8 0.0 copy-start.6
  228.8 2.1 copy-done.8
  230.8 0.0 copy-done.9
  230.8 3.7 fusion
  234.5 0.0 copy-done.6
  234.5 1.4 copy.57
  235.9 38.6 %all_to_all.65 = bf16[2,8,512,128]{3,1,0,2:T(8,128)(2,1)S(1)} all-to-all(bf16[2,8,512,128]{3,1,0,2:T(8,128)(2,1)S(1)} %copy.57), channel_id=1, replica_groups=mesh['dp'=4,'seq'=64] {'seq'}, dimensions={2} | all-to-all | bytes 4194304 | tf_op jit(solution)/shard_map/all_to_all | solution.py:29
  274.5 0.8 copy.59
  275.3 0.0 copy-start.4
  275.3 1.3 copy-done.4
  276.7 3.3 bitcast_convert_fusion
  280.0 0.0 reduce-scatter.5.cloned.1.call-update
  280.0 0.0 reduce-scatter.3.cloned.1.call-start
  280.0 1.5 copy-done.5
  281.6 4.8 %convert_bitcast_fusion.1 = bf16[2,512,8,128]{1,3,0,2:T(8,128)(2,1)} fusion(bf16[8,512,512]{2,1,0:T(8,128)(2,1)} %all-gather.5.cloned.1.call-done, bf16[2,512,8,128]{3,2,1,0:T(8,128)(2,1)S(1)} %bitcast.97), kind=kOutput, calls=%fused_computation.31 | convolution fusion | flops 1074790400 | bytes 8388608 | tf_op jit(solution)/shard_map/qij,tiqc->tjqc/dot_general | solution.py:30
  286.4 4.9 %copy.61 = bf16[2,512,8,128]{3,0,2,1:T(2,128)(2,1)S(1)} copy(bf16[2,512,8,128]{1,3,0,2:T(8,128)(2,1)} %convert_bitcast_fusion.1) | data formatting | bytes 4194304 | tf_op jit(solution)/shard_map/convert_element_type | solution.py:31
  291.3 53.9 %all_to_all.66 = bf16[2,512,8,128]{3,0,2,1:T(2,128)(2,1)S(1)} all-to-all(bf16[2,512,8,128]{3,0,2,1:T(2,128)(2,1)S(1)} %copy.61), channel_id=1, replica_groups=mesh['dp'=4,'seq'=64] {'seq'}, dimensions={1} | all-to-all | bytes 4194304 | tf_op jit(solution)/shard_map/all_to_all | solution.py:32
  345.2 0.3 copy.62
  345.5 1.3 copy-done.3
  346.8 3.3 bitcast_convert_fusion.1
  350.1 0.0 reduce-scatter.3.cloned.1.call-update
  350.1 6.0 %fusion.14 = f32[2,8,512,128]{3,2,1,0:T(8,128)} fusion(bf16[8,512,512]{2,1,0:T(8,128)(2,1)} %all-gather.3.cloned.1.call-done, bf16[2,8,64,8,128]{4,3,1,2,0:T(8,128)(2,1)S(1)} %bitcast.95, bf16[128,128]{1,0:T(8,128)(2,1)S(1)} %copy-done.7), kind=kOutput, calls=%fused_computation.22 | convolution fusion | flops 1343225856 | bytes 10518528 | tf_op jit(solution)/shard_map/tpqd,cd->tpqc/dot_general | solution.py:39
  356.1 8.3 %add_convert_fusion = bf16[2,8,512,128]{3,2,1,0:T(8,128)(2,1)} fusion(f32[2,8,512,128]{3,2,1,0:T(8,128)} %fusion.14, bf16[2,8,512,128]{3,2,1,0:T(8,128)(2,1)} %param.11, f32[2,8,512,128]{3,2,1,0:T(8,128)} %get-tuple-element.6, bf16[128,128]{1,0:T(8,128)(2,1)S(1)} %copy-done.9, bf16[2,64,8,8,128]{4,3,2,1,0:T(8,128)(2,1)} %bitcast.101), kind=kOutput, calls=%fused_computation.19 | convolution fusion | flops 283115520 | bytes 14712832 | tf_op jit(solution)/shard_map/tpqd,cd->tpqc/dot_general | solution.py:41
  364.4 21.3 %reduce-scatter.5.cloned.1.call-done = bf16[8,128,512]{2,1,0:T(8,128)(2,1)} async-done(((bf16[8,512,512]{2,1,0:T(8,128)(2,1)}), bf16[8,128,512]{2,1,0:T(8,128)(2,1)}) %reduce-scatter.5.cloned.1.call-update) | async-done | bytes 1048592 | tf_op jit(solution)/shard_map/reduce_scatter | solution.py:47
  385.6 2.4 multiply_convert_fusion
  388.0 49.5 %reduce-scatter.3.cloned.1.call-done = bf16[8,128,512]{2,1,0:T(8,128)(2,1)} async-done(((bf16[8,512,512]{2,1,0:T(8,128)(2,1)}), bf16[8,128,512]{2,1,0:T(8,128)(2,1)}) %reduce-scatter.3.cloned.1.call-update) | async-done | bytes 1048592 | tf_op jit(solution)/shard_map/reduce_scatter | solution.py:51
  437.6 2.4 multiply_convert_fusion.1
  440.0 0.0 copy-done.1
  (8 shorter events, 0.0 us)
Async XLA Ops:
  7.2 1.6 copy-start
  7.2 1.6 copy-start.7
  7.2 56.1 %all-gather.3.cloned.1.call-start = ((), (), s32[]{:S(2)}) async-start(), calls=%async_computation.6 | async-start | bytes 5242880 | tf_op jit(solution)/shard_map/all_gather | solution.py:9
  7.9 157.9 %all-gather.5.cloned.1.call-start = ((), (), s32[]{:S(2)}) async-start(), calls=%async_computation.7 | async-start | bytes 5242880 | tf_op jit(solution)/shard_map/all_gather | solution.py:10
  8.7 377.0 %reduce-scatter.5.cloned.1.call-start = ((), (), s32[]{:S(2)}) async-start(), calls=%async_computation.9 | async-start | bytes 5242880 | tf_op jit(solution)/shard_map/reduce_scatter | solution.py:47
  228.5 2.3 copy-start.8
  228.5 2.3 copy-start.9
  228.8 5.8 %copy-start.6 = (bf16[2,512,8,128]{3,2,1,0:T(8,128)(2,1)}, bf16[2,512,8,128]{3,2,1,0:T(8,128)(2,1)S(1)}, u32[]{:S(2)}) copy-start(bf16[2,512,8,128]{3,2,1,0:T(8,128)(2,1)S(1)} %copy.55) | copy-start | bytes 6291460
  274.5 2.2 copy-start.2
  275.3 1.3 copy-start.4
  280.0 1.6 copy-start.5
  280.0 157.6 %reduce-scatter.3.cloned.1.call-start = ((), (), s32[]{:S(2)}) async-start(), calls=%async_computation.8 | async-start | bytes 5242880 | tf_op jit(solution)/shard_map/reduce_scatter | solution.py:51
  345.2 1.6 copy-start.3
  356.1 83.9 %copy-start.1 = (bf16[2,8,512,128]{3,2,1,0:T(8,128)(2,1)S(1)}, bf16[2,8,512,128]{3,2,1,0:T(8,128)(2,1)}, u32[]{:S(2)}) copy-start(bf16[2,8,512,128]{3,2,1,0:T(8,128)(2,1)} %param.6) | copy-start | bytes 6291460
Sparse Core Ops, SparseCore 0:
  9.8 53.3 all-gather.2
  65.1 94.5 all-gather.4
  280.1 105.4 reduce-scatter.4
  388.2 49.3 reduce-scatter.2
where the time goes:
time: 448 us; the launch traced here: 447 us
  blocking collectives  232 us (52%)
  waiting for transfers between devices  125 us (28%)
  matrix products  42.5 us (9%)
  local copies, waits for them, and re-layouts  28.8 us (6%)
  between operations  13.8 us (3%)
  other arithmetic  4.8 us (1%)
    all_to_all x1, blocking collectives, on_device(): lax.all_to_all(rowmix, 'seq', split_axis=2, concat_axis=1, tiled=True)  88.4 us
    all_to_all x1, blocking collectives, on_device(): lax.all_to_all(d_row_cols, 'seq', split_axis=1, concat_axis=2, tiled=True)  53.9 us
    all_gather x1, waiting for transfers between devices, on_device(): lax.all_gather(first_blocks, 'dp', axis=1, tiled=True)  52.5 us
    all_to_all x1, blocking collectives, on_device(): lax.all_to_all(colmix_cols, 'seq', split_axis=1, concat_axis=2, tiled=True)  50.9 us
    reduce_scatter x1, waiting for transfers between devices, on_device(): lax.psum_scatter(first_part.astype(jnp.bfloat16), 'dp', scatter_dimension...  49.5 us
    all_to_all x1, blocking collectives, on_device(): lax.all_to_all(d_col, 'seq', split_axis=2, concat_axis=1, tiled=True)  38.6 us
    reduce_scatter x1, waiting for transfers between devices, on_device(): lax.psum_scatter(second_part.astype(jnp.bfloat16), 'dp', scatter_dimensio...  21.3 us
  transfers between devices with their start and end apart: 4, of which 3 were waited for; matrix products, arithmetic and copies ran while one was open for 10% of the time, Pallas kernels for 0%

commit v1 on v0

v1 whole, which is shorter than its diff:
```python
import jax
import jax.numpy as jnp
from jax import lax
from jax.experimental import pallas as pl
from jax.experimental.pallas import tpu as pltpu
from jax.sharding import PartitionSpec as P

MESH = pl.DeviceIdType.MESH
BF = jnp.bfloat16
F32 = jnp.float32


def exchange_kernel(x_ref, o_ref, send_sem, recv_sem, own_sem):
    n = x_ref.shape[0]
    width = lax.axis_size("dp")
    me = lax.axis_index("seq") * width + lax.axis_index("dp")

    def device(k):
        d = lax.rem(me + k, n)
        return d, (lax.rem(d, width), d // width)

    barrier = pltpu.get_barrier_semaphore()

    def greet(k, carry):
        pl.semaphore_signal(barrier, inc=1, device_id=device(k)[1], device_id_type=MESH)
        return carry

    lax.fori_loop(1, n, greet, 0)
    own = pltpu.make_async_copy(x_ref.at[me], o_ref.at[me], own_sem)
    own.start()
    pl.semaphore_wait(barrier, n - 1)

    def send(k, carry):
        d, where = device(k)
        pltpu.make_async_remote_copy(
            x_ref.at[d], o_ref.at[me], send_sem, recv_sem, device_id=where, device_id_type=MESH
        ).start()
        return carry

    lax.fori_loop(1, n, send, 0)
    own.wait()
    rest = pl.ds(0, n - 1)
    pltpu.make_async_copy(x_ref.at[rest], o_ref.at[rest], recv_sem).wait()
    pltpu.make_async_copy(x_ref.at[rest], o_ref.at[rest], send_sem).wait()


def exchange(x):
    return pl.pallas_call(
        exchange_kernel,
        out_shape=jax.ShapeDtypeStruct(x.shape, x.dtype),
        in_specs=[pl.BlockSpec(memory_space=pltpu.VMEM)],
        out_specs=pl.BlockSpec(memory_space=pltpu.VMEM),
        scratch_shapes=[pltpu.SemaphoreType.DMA] * 3,
        cost_estimate=pl.CostEstimate(flops=0, bytes_accessed=150_000_000, transcendentals=0),
        compiler_params=pltpu.CompilerParams(
            collective_id=1, has_side_effects=True, vmem_limit_bytes=16 << 20
        ),
    )(x)


def on_device(traces_in, w_value, w_gate, first_blocks, second_blocks, cotangent):
    dp, seq = lax.axis_size("dp"), lax.axis_size("seq")
    n = dp * seq
    traces, rows, columns, channels = traces_in.shape
    mine = columns // n

    def to_columns(x):
        x = x.reshape(traces, rows, n, mine, channels).transpose(2, 0, 3, 1, 4)
        x = exchange(x.reshape(n, traces * mine, rows, channels))
        return x.reshape(seq, dp, traces, mine, rows, channels)

    def to_rows(x):
        x = exchange(x.reshape(n, traces * mine, rows, channels))
        x = x.reshape(n, traces, mine, rows, channels).transpose(1, 3, 0, 2, 4)
        return x.reshape(traces, rows, columns, channels)

    gates = jnp.einsum("tpqc,cd->tpqd", traces_in, w_gate, preferred_element_type=F32)
    sig = jax.nn.sigmoid(gates)
    act = gates * sig
    gradf = cotangent.astype(F32)
    d_col = (gradf * act).astype(BF)
    full_first = lax.all_gather(first_blocks, "dp", axis=1, tiled=True)
    cotan_cols = to_columns(d_col)
    values = jnp.einsum("tpqc,cd->tpqd", traces_in, w_value, preferred_element_type=F32).astype(BF)
    rowmix = jnp.einsum("pij,tpjc->tpic", full_first, values, preferred_element_type=F32).astype(BF)
    rowmix, cotan_cols = lax.optimization_barrier((rowmix, cotan_cols))
    second = lax.all_to_all(second_blocks, "dp", split_axis=0, concat_axis=1, tiled=True)
    cols = to_columns(rowmix)
    split = second.reshape(mine, seq, rows, columns)
    split_j = second.reshape(mine, columns, seq, rows)
    d_row_cols = jnp.einsum("qspj,sdtqpc->qjdtc", split, cotan_cols, preferred_element_type=F32).astype(BF)

    def chunks(x):
        x = x.reshape(mine, seq, rows, dp, traces, channels)
        return x.transpose(1, 3, 4, 0, 2, 5)

    d_row_chunks, cols = lax.optimization_barrier((chunks(d_row_cols), cols))
    d_row = to_rows(d_row_chunks)
    colmix_cols = jnp.einsum("qisp,sdtqpc->qidtc", split_j, cols, preferred_element_type=F32).astype(BF)
    colmix_chunks, d_row = lax.optimization_barrier((chunks(colmix_cols), d_row))
    first_part = jnp.einsum("tpic,tpjc->pij", d_row, values, preferred_element_type=F32)
    first_sum = lax.psum_scatter(first_part.astype(BF), "dp", scatter_dimension=1, tiled=True)
    trace_count = traces * dp
    grad_first = (first_sum.astype(F32) / trace_count).astype(BF)
    colmix = to_rows(colmix_chunks)
    grad_second = jnp.einsum(
        "sdtqpc,SdtqPc->qspSP", cotan_cols, cols, preferred_element_type=F32
    ).reshape(mine, columns, columns)
    grad_second = (grad_second / trace_count).astype(BF)
    grad_second = lax.all_to_all(grad_second, "dp", split_axis=1, concat_axis=0, tiled=True)
    colf = colmix.astype(F32)
    mixed = (colf * act).astype(BF)
    d_gate = (gradf * colf * sig * (1.0 + gates * (1.0 - sig))).astype(BF)
    d_val = jnp.einsum("pij,tpic->tpjc", full_first, d_row, preferred_element_type=F32).astype(BF)
    grad_in = jnp.einsum("tpqd,cd->tpqc", d_val, w_value, preferred_element_type=F32)
    grad_in = (
        grad_in + jnp.einsum("tpqd,cd->tpqc", d_gate, w_gate, preferred_element_type=F32)
    ).astype(BF)
    return (mixed, grad_in, grad_first, grad_second)


def solution(mesh):
    big, weight = P("dp", "seq", None, None), P("seq", "dp", None)
    return jax.shard_map(
        on_device,
        mesh=mesh,
        in_specs=(big, P(), P(), weight, weight, big),
        out_specs=(big, big, weight, weight),
        check_vma=False,
    )
```

time: 448 us -> 428 us (0.955)
  Pallas kernels: 0 us -> 282 us
  blocking collectives: 232 us -> 0 us
  waiting for transfers between devices: 125 us -> 0.72 us
  local copies, waits for them, and re-layouts: 28.8 us -> 71.7 us
  starting transfers between devices: 0.16 us -> 10.3 us
    pallas_call x0 -> x4, Pallas kernels: none -> 282 us  [exchange(): pl.pallas_call(exchange_kernel, out_shape=jax.ShapeDtypeStruct(x.shape, x...]
    all_to_all x4 -> x0, blocking collectives: 232 us -> none  [the longest x1 88.4 us: on_device(): lax.all_to_all(rowmix, 'seq', split_axis=2, concat_axis=1, tiled=True)]
    reduce_scatter x2 -> x1, waiting for transfers between devices: 70.8 us -> 0.01 us  [on_device(): lax.psum_scatter(first_part.astype(BF), 'dp', scatter_dimension=1, tiled=...]
    all_gather x2 -> x1, waiting for transfers between devices: 52.5 us -> 0.02 us  [on_device(): full_first = lax.all_gather(first_blocks, 'dp', axis=1, tiled=True)]
    convert_element_type x4 -> x5, local copies, waits for them, and re-layouts: 18.6 us -> 47.2 us  [the longest x2 34.8 us: on_device(): grad_second = (grad_second / trace_count).astype(BF)]
    all_to_all x0 -> x2, starting transfers between devices: none -> 10.2 us  [the longest x1 6.73 us: on_device(): lax.all_to_all(second_blocks, 'dp', split_axis=0, concat_axis=1, tiled=True)]
    optimization_barrier x0 -> x3, local copies, waits for them, and re-layouts: none -> 7.53 us  [the longest x1 3.18 us: on_device(): rowmix, cotan_cols = lax.optimization_barrier((rowmix, cotan_cols))]
    convert_element_type x2 -> x3, other arithmetic: 4.8 us -> 8.99 us  [the longest x1 6.01 us: on_device(): mixed = (colf * act).astype(BF)]
  transfers between devices with their start and end apart: 4 -> 4, of which waited for: 3 -> 0; matrix products, arithmetic and copies ran while one was open for 10% -> 19% of each run, Pallas kernels for 0% -> 39%
where the time goes in v1:
time: 428 us; the launch traced here: 427 us
  Pallas kernels  282 us (66%)
  local copies, waits for them, and re-layouts  71.7 us (17%)
  matrix products  38.7 us (9%)
  between operations  14.3 us (3%)
  starting transfers between devices  10.3 us (2%)
  other arithmetic  8.99 us (2%)
    pallas_call x4, Pallas kernels, exchange(): pl.pallas_call(exchange_kernel, out_shape=jax.ShapeDtypeStruct(x.shape, x...  282 us
    convert_element_type x2, local copies, waits for them, and re-layouts, on_device(): grad_second = (grad_second / trace_count).astype(BF)  34.8 us
    dot_general x1, matrix products, on_device(): jnp.einsum('tpqd,cd->tpqc', d_gate, w_gate, preferred_element_type=F32)  8.66 us
  transfers between devices with their start and end apart: 4, of which 0 were waited for; matrix products, arithmetic and copies ran while one was open for 19% of the time, Pallas kernels for 39%

profile of v1, /device:TPU:1, one launch (start us, length us, event | category | flops | bytes accessed | tf_op | source)
XLA Modules:
  0.0 426.6 jit_solution(6632786167936035340)
XLA Ops:
  7.2 0.0 copy-start
  7.2 0.0 all-gather.2.cloned.1.call-start
  7.2 0.7 all-gather.2.cloned.1.call-update
  7.9 6.7 %all-to-all-start = ((bf16[8,128,512]{2,1,0:T(8,128)(2,1)}), bf16[8,128,512]{2,1,0:T(8,128)(2,1)S(1)}, u32[]{:S(2)}, u32[]{:S(2)}) async-start(bf16[8,128,512]{2,1,0:T(8,128)(2,1)} %param.10), calls=%async_computation | async-start | bytes 2097152 | tf_op jit(solution)/shard_map/all_to_all | solution.py:87
  14.7 4.8 %fusion = (bf16[2,8,512,128]{3,2,1,0:T(8,128)(2,1)S(1)}, f32[2,8,512,128]{3,2,1,0:T(8,128)}) fusion(bf16[2,8,512,128]{3,2,1,0:T(8,128)(2,1)} %param.11, bf16[2,8,512,128]{3,2,1,0:T(8,128)(2,1)S(1)} %copy-done, bf16[128,128]{1,0:T(8,128)(2,1)S(1)} %copy-done.11), kind=kOutput, calls=%fused_computation.3 | convolution fusion | flops 275775488 | bytes 10518528 | tf_op jit(solution)/shard_map/tpqc,cd->tpqd/dot_general | solution.py:77
  19.5 2.4 copy.63
  21.9 83.3 %shard_map.93 = bf16[256,4,8,128]{3,2,1,0:T(8,128)(2,1)S(1)} custom-call(bf16[256,4,8,128]{3,2,1,0:T(8,128)(2,1)S(1)} %bitcast.115), custom_call_target="tpu_custom_call" | custom-call | bytes 150000000 | tf_op jit(solution)/shard_map/pallas_call | solution.py:48
  105.2 1.3 copy-done.2
  106.6 2.0 convolution_convert_fusion
  108.6 1.4 copy.70
  110.0 1.1 copy.64
  111.1 1.5 reshape.70
  112.6 0.0 all-gather.2.cloned.1.call-done
  112.6 4.9 %convert_bitcast_fusion.1 = bf16[2,8,512,128]{2,3,0,1:T(8,128)(2,1)} fusion(bf16[8,512,512]{2,1,0:T(8,128)(2,1)} %all-gather.2.cloned.1.call-done, bf16[2,8,512,128]{3,2,1,0:T(8,128)(2,1)S(1)} %copy-done.8), kind=kOutput, calls=%fused_computation.33 | convolution fusion | flops 1074790400 | bytes 8388608 | tf_op jit(solution)/shard_map/pij,tpjc->tpic/dot_general | solution.py:85
  117.5 3.2 copy.68
  120.6 0.4 copy.69
  121.0 0.0 copy-start.9
  121.0 58.4 %shard_map.94 = bf16[256,4,8,128]{3,2,1,0:T(8,128)(2,1)S(1)} custom-call(bf16[256,4,8,128]{3,2,1,0:T(8,128)(2,1)S(1)} %bitcast.116), custom_call_target="tpu_custom_call" | custom-call | bytes 150000000 | tf_op jit(solution)/shard_map/pallas_call | solution.py:48
  179.5 0.0 copy-start.4
  179.5 1.3 copy-done.4
  180.8 1.3 fusion.19
  182.1 1.5 copy.145
  183.6 4.1 copy.67
  187.7 2.2 copy.74
  189.9 59.0 %shard_map.95 = bf16[256,4,8,128]{3,2,1,0:T(8,128)(2,1)S(1)} custom-call(bf16[256,4,8,128]{3,2,1,0:T(8,128)(2,1)S(1)} %bitcast.117), custom_call_target="tpu_custom_call" | custom-call | bytes 150000000 | tf_op jit(solution)/shard_map/pallas_call | solution.py:48
  248.9 0.0 copy-start.5
  248.9 3.2 copy.75
  252.1 1.3 fusion.17
  253.4 1.5 copy.146
  254.9 4.2 copy.73
  259.1 5.5 %bitcast_convert_fusion = bf16[8,512,512]{2,1,0:T(8,128)(2,1)} fusion(bf16[2,8,512,128]{3,2,0,1:T(8,128)(2,1)} %bitcast.124, bf16[2,8,512,128]{3,2,1,0:T(8,128)(2,1)} %convolution_convert_fusion), kind=kOutput, calls=%fused_computation | convolution fusion | flops 1075838976 | bytes 8388608 | tf_op jit(solution)/shard_map/tpic,tpjc->pij/dot_general | solution.py:101
  264.6 0.0 reduce-scatter.2.cloned.1.call-update
  264.6 2.2 copy.76
  266.8 81.3 %shard_map.96 = bf16[256,4,8,128]{3,2,1,0:T(8,128)(2,1)S(1)} custom-call(bf16[256,4,8,128]{3,2,1,0:T(8,128)(2,1)S(1)} %bitcast.119), custom_call_target="tpu_custom_call" | custom-call | bytes 150000000 | tf_op jit(solution)/shard_map/pallas_call | solution.py:48
  348.1 0.6 convert_bitcast_fusion
  348.7 0.0 copy-start.6
  348.7 4.1 copy.77
  352.8 4.3 %fusion.4 = bf16[2,64,8,64,8]{3,2,4,1,0:T(8,128)(2,1)} fusion(bf16[64,4,2,2,8,128,1]{5,4,3,2,1,0,6:T(8,128)(2,1)S(1)} %bitcast.123, bf16[64,4,2,2,8,128]{5,4,3,2,1,0:T(8,128)(2,1)S(1)} %bitcast.121), kind=kOutput, calls=%fused_computation.8 | convolution fusion | flops 1074790400 | bytes 5242880 | tf_op jit(solution)/shard_map/sdtqpc,SdtqPc->qspSP/dot_general | solution.py:106
  357.1 12.6 %copy.115 = bf16[2,64,8,64,8]{4,3,0,2,1:T(8,128)(2,1)} copy(bf16[2,64,8,64,8]{3,2,4,1,0:T(8,128)(2,1)} %fusion.4) | data formatting | bytes 2097152 | tf_op jit(solution)/shard_map/convert_element_type | solution.py:109
  369.7 22.2 %reshape.89 = bf16[2,512,512]{2,0,1:T(2,128)(2,1)} reshape(bf16[2,64,8,64,8]{4,3,0,2,1:T(8,128)(2,1)} %copy.115) | data formatting | bytes 2097152 | tf_op jit(solution)/shard_map/convert_element_type | solution.py:109
  391.9 3.5 all-to-all-start.1
  395.4 6.0 %multiply_convert_fusion = bf16[2,8,512,128]{3,2,1,0:T(8,128)(2,1)} fusion(f32[2,8,512,128]{3,2,1,0:T(8,128)} %bitcast.126, f32[2,8,512,128]{3,2,1,0:T(8,128)} %get-tuple-element.17), kind=kLoop, calls=%fused_computation.17 | loop fusion | flops 6291456 | bytes 10485760 | tf_op jit(solution)/shard_map/convert_element_type | solution.py:112
  401.4 6.0 %fusion.14 = f32[2,8,512,128]{3,2,1,0:T(8,128)} fusion(bf16[8,512,512]{2,1,0:T(8,128)(2,1)} %all-gather.2.cloned.1.call-done, bf16[2,8,512,128]{3,2,0,1:T(8,128)(2,1)S(1)} %bitcast.125, bf16[128,128]{1,0:T(8,128)(2,1)S(1)} %copy-done.10), kind=kOutput, calls=%fused_computation.24 | convolution fusion | flops 1343225856 | bytes 10518528 | tf_op jit(solution)/shard_map/tpqd,cd->tpqc/dot_general | solution.py:115
  407.4 8.7 %add_convert_fusion = bf16[2,8,512,128]{3,2,1,0:T(8,128)(2,1)} fusion(f32[2,8,512,128]{3,2,1,0:T(8,128)} %fusion.14, f32[2,8,512,128]{3,2,1,0:T(8,128)} %bitcast.127, bf16[2,8,512,128]{3,2,1,0:T(8,128)(2,1)} %param.11, f32[2,8,512,128]{3,2,1,0:T(8,128)} %get-tuple-element.17, bf16[128,128]{1,0:T(8,128)(2,1)S(1)} %copy-done.11), kind=kOutput, calls=%fused_computation.16 | convolution fusion | flops 282066944 | bytes 16809984 | tf_op jit(solution)/shard_map/tpqd,cd->tpqc/dot_general | solution.py:117
  416.1 0.2 copy.85
  416.2 0.0 copy-start.1
  416.3 1.1 copy.86
  417.3 2.4 multiply_convert_fusion.1
  (20 shorter events, 0.0 us)
Async XLA Ops:
  7.2 7.5 %copy-start = (bf16[2,8,512,128]{3,2,1,0:T(8,128)(2,1)S(1)}, bf16[2,8,512,128]{3,2,1,0:T(8,128)(2,1)}, u32[]{:S(2)}) copy-start(bf16[2,8,512,128]{3,2,1,0:T(8,128)(2,1)} %param.6) | copy-start | bytes 6291460
  7.2 7.5 %copy-start.11 = (bf16[128,128]{1,0:T(8,128)(2,1)S(1)}, bf16[128,128]{1,0:T(8,128)(2,1)}, u32[]{:S(2)}) copy-start(bf16[128,128]{1,0:T(8,128)(2,1)} %param.8) | copy-start | bytes 98308
  7.2 105.4 %all-gather.2.cloned.1.call-start = ((), (), s32[]{:S(2)}) async-start(), calls=%async_computation.3 | async-start | bytes 5242880 | tf_op jit(solution)/shard_map/all_gather | solution.py:82
  7.9 100.6 %all-to-all-start = ((bf16[8,128,512]{2,1,0:T(8,128)(2,1)}), bf16[8,128,512]{2,1,0:T(8,128)(2,1)S(1)}, u32[]{:S(2)}, u32[]{:S(2)}) async-start(bf16[8,128,512]{2,1,0:T(8,128)(2,1)} %param.10), calls=%async_computation | async-start | bytes 2097152 | tf_op jit(solution)/shard_map/all_to_all | solution.py:87
  14.7 402.7 %reduce-scatter.2.cloned.1.call-start = ((), (), s32[]{:S(2)}) async-start(), calls=%async_computation.4 | async-start | bytes 5242880 | tf_op jit(solution)/shard_map/reduce_scatter | solution.py:102
  21.9 84.6 %copy-start.10 = (bf16[128,128]{1,0:T(8,128)(2,1)S(1)}, bf16[128,128]{1,0:T(8,128)(2,1)}, u32[]{:S(2)}) copy-start(bf16[128,128]{1,0:T(8,128)(2,1)} %param.7) | copy-start | bytes 98308
  105.2 1.3 copy-start.2
  110.0 2.6 copy-start.8
  121.0 59.8 %copy-start.3 = (bf16[256,4,8,128]{3,2,1,0:T(8,128)(2,1)S(1)}, bf16[256,4,8,128]{3,2,1,0:T(8,128)(2,1)}, u32[]{:S(2)}) copy-start(bf16[256,4,8,128]{3,2,1,0:T(8,128)(2,1)} %copy-done.2) | copy-start | bytes 6291460
  121.0 59.8 %copy-start.9 = (bf16[2,4,128,512]{3,2,1,0:T(8,128)(2,1)S(1)}, bf16[2,4,128,512]{3,2,1,0:T(8,128)(2,1)}, u32[]{:S(2)}) copy-start(bf16[2,4,128,512]{3,2,1,0:T(8,128)(2,1)} %copy.64) | copy-start | bytes 3145732
  179.5 1.3 copy-start.4
  248.9 3.2 copy-start.5
  348.7 4.1 copy-start.6
  391.9 24.2 %all-to-all-start.1 = ((bf16[2,512,512]{2,0,1:T(2,128)(2,1)}), bf16[2,512,512]{2,0,1:T(2,128)(2,1)S(1)}, u32[]{:S(2)}, u32[]{:S(2)}) async-start(bf16[2,512,512]{2,0,1:T(2,128)(2,1)} %reshape.89), calls=%async_computation.2 | async-start | bytes 2097152 | tf_op jit(solution)/shard_map/all_to_all | solution.py:110
  395.4 6.0 %copy-start.7 = (bf16[2,8,256,2,128]{4,3,2,0,1:T(2,128)(2,1)S(1)}, bf16[2,8,256,2,128]{4,3,2,0,1:T(2,128)(2,1)}, u32[]{:S(2)}) copy-start(bf16[2,8,256,2,128]{4,3,2,0,1:T(2,128)(2,1)} %copy.75) | copy-start | bytes 6291460
  416.2 3.5 copy-start.1
Sparse Core Ops, SparseCore 0:
  9.8 98.3 all-gather.1
  264.7 91.7 reduce-scatter.1

commit v2 on v0

v2 whole, which is shorter than its diff:
```python
import jax
import jax.numpy as jnp
from jax import lax
from jax.experimental import pallas as pl
from jax.experimental.pallas import tpu as pltpu
from jax.sharding import PartitionSpec as P

MESH = pl.DeviceIdType.MESH
BF = jnp.bfloat16
F32 = jnp.float32
NT = (((1,), (1,)), ((), ()))
TN = (((0,), (0,)), ((), ()))
NN = (((1,), (0,)), ((), ()))


def dot(a, b, dims=NN):
    return lax.dot_general(a, b, dims, preferred_element_type=F32)


def kernel(
    x_hbm, wv_hbm, wg_hbm, first_hbm, second_hbm, cot_hbm,
    mixed_hbm, gin_hbm, gf_hbm, gs_hbm,
    x, wv, wg, cot, val, act, slope, part, first, second, tmp,
    send_a, send_b, cols_a, cols_b, send_c, send_d, rows_c, rows_d,
    gf_tmp, gf_own, gf_near, gf_near_in, gf_far, gf_far_in, gs,
    in_sem, f_send, f_recv, s_send, s_recv, ex_send, ex_recv, ex_own,
    near_send, near_recv, far_send, far_recv, gs_send, gs_recv, gs_own, out_sem,
):
    width, length = lax.axis_size("dp"), lax.axis_size("seq")
    n = width * length
    traces, rows, columns, channels = x.shape
    mine = columns // n
    share = columns // width
    d, s = lax.axis_index("dp"), lax.axis_index("seq")
    me = s * width + d
    near = d + 1 - 2 * lax.rem(d, 2)
    far = lax.rem(d + 2, width)
    cross = lax.rem(near + 2, width)

    loads = [
        pltpu.make_async_copy(a, b, in_sem.at[i])
        for i, (a, b) in enumerate(
            [
                (x_hbm, x), (cot_hbm, cot), (wg_hbm, wg), (wv_hbm, wv),
                (first_hbm, first.at[:, pl.ds(pl.multiple_of(share * d, share), share), :]),
                (
                    second_hbm.at[pl.ds(mine * d, mine)],
                    second.at[:, pl.ds(pl.multiple_of(share * d, share), share), :],
                ),
            ]
        )
    ]
    for load in loads:
        load.start()

    barrier = pltpu.get_barrier_semaphore()

    def greet(k, carry):
        e = lax.rem(me + k, n)
        pl.semaphore_signal(
            barrier, inc=1, device_id=(lax.rem(e, width), e // width), device_id_type=MESH
        )
        return carry

    lax.fori_loop(1, n, greet, 0)
    pl.semaphore_wait(barrier, n - 1)

    def remote(a, b, send, recv, to_dp, to_seq):
        return pltpu.make_async_remote_copy(
            a, b, send, recv, device_id=(to_dp, to_seq), device_id_type=MESH
        )

    def block(owner):
        return pl.ds(pl.multiple_of(share * owner, share), share)

    first_far = remote(first_hbm, first.at[:, block(d), :], f_send.at[0], f_recv.at[0], far, s)
    first_near = remote(first_hbm, first.at[:, block(d), :], f_send.at[1], f_recv.at[1], near, s)
    first_pass = remote(
        first.at[:, block(far), :], first.at[:, block(far), :], f_send.at[2], f_recv.at[2], near, s
    )
    first_far.start()
    first_near.start()

    def pieces_wait(sem):
        rest = send_a.at[:, pl.ds(0, columns - mine)]
        pltpu.make_async_copy(rest, rest, sem).wait()

    def to_columns(buf, out, which):
        def target(o):
            return o.at[pl.ds(traces * d, traces), :, pl.ds(pl.multiple_of(rows * s, rows), rows), :]

        own = pltpu.make_async_copy(
            buf.at[:, pl.ds(mine * me, mine)], target(out), ex_own.at[which]
        )
        own.start()

        def send(k, carry):
            e = lax.rem(me + k, n)
            remote(
                buf.at[:, pl.ds(mine * e, mine)], target(out),
                ex_send.at[which], ex_recv.at[which], lax.rem(e, width), e // width,
            ).start()
            return carry

        lax.fori_loop(1, n, send, 0)
        return own

    def source(buf, e_dp, e_seq):
        return buf.at[
            pl.ds(traces * e_dp, traces), :, pl.ds(pl.multiple_of(rows * e_seq, rows), rows), :
        ]

    def to_rows(buf, out, which, e_dp, first_k):
        def send(k, carry):
            e_seq = lax.rem(s + k, length)
            remote(
                source(buf, e_dp, e_seq), out.at[:, pl.ds(mine * me, mine)],
                ex_send.at[which], ex_recv.at[which], e_dp, e_seq,
            ).start()
            return carry

        lax.fori_loop(first_k, length, send, 0)

    step = 64

    def pack(buf):
        def body(i, carry):
            t, k = i // (columns // step), lax.rem(i, columns // step)
            rows_here = pl.ds(pl.multiple_of(k * step * rows, step * rows), step * rows)
            y = tmp[t, rows_here, :].reshape(step, rows, channels)
            buf[t, pl.ds(k * step, step)] = y.astype(BF)
            return carry

        lax.fori_loop(0, traces * (columns // step), body, 0)

    def unpack(buf):
        def body(i, carry):
            t, k = i // (columns // step), lax.rem(i, columns // step)
            rows_here = pl.ds(pl.multiple_of(k * step * rows, step * rows), step * rows)
            y = buf[t, pl.ds(k * step, step)].astype(F32)
            tmp[t, rows_here, :] = y.reshape(step * rows, channels)
            return carry

        lax.fori_loop(0, traces * (columns // step), body, 0)

    def row(p):
        return pl.ds(p, columns, stride=rows)

    loads[0].wait()
    loads[1].wait()
    loads[2].wait()

    def gate(i, carry):
        t, p = i // rows, lax.rem(i, rows)
        g = dot(x[t, p], wg[...])
        sig = jax.nn.sigmoid(g)
        a = g * sig
        c = cot[t, p].astype(F32)
        act[t, p] = a
        slope[t, p] = c * sig * (1.0 + g * (1.0 - sig))
        tmp[t, row(p), :] = c * a
        return carry

    lax.fori_loop(0, traces * rows, gate, 0)
    pack(send_a)
    own_a = to_columns(send_a, cols_a, 0)

    def second_to(other):
        return remote(
            second_hbm.at[pl.ds(mine * other, mine)], second.at[:, block(d), :],
            s_send, s_recv, other, s,
        )

    for other in (far, cross, near):
        second_to(other).start()

    loads[3].wait()

    def value(i, carry):
        t, p = i // rows, lax.rem(i, rows)
        val[t, p] = dot(x[t, p], wv[...]).astype(BF)
        return carry

    lax.fori_loop(0, traces * rows, value, 0)

    loads[4].wait()
    first_far.wait_recv()
    first_pass.start()
    first_near.wait_recv()
    first_pass.wait_recv()

    def both(ref, p):
        return jnp.concatenate([ref[t, p] for t in range(traces)], axis=1)

    def mix_rows(p, carry):
        o = dot(first[p], both(val, p))
        for t in range(traces):
            tmp[t, row(p), :] = o[:, t * channels : (t + 1) * channels]
        return carry

    lax.fori_loop(0, rows, mix_rows, 0)
    pack(send_b)
    own_b = to_columns(send_b, cols_b, 1)

    loads[5].wait()
    half = second.at[:, pl.ds(0, share * (width - 1)), :]
    pltpu.make_async_copy(half, half, s_recv).wait()

    def columns_back(cols, buf, out, which, dims):
        owns = []
        for k in range(width):
            e_dp = lax.rem(d + k, width)

            def mix(q, carry):
                r = jnp.concatenate(
                    [cols[traces * e_dp + t, q] for t in range(traces)], axis=1
                )
                o = dot(second[q], r, dims).astype(BF)
                for t in range(traces):
                    buf[traces * e_dp + t, q] = o[:, t * channels : (t + 1) * channels]
                return carry

            lax.fori_loop(0, mine, mix, 0)
            if k == 0:
                own = pltpu.make_async_copy(
                    source(buf, d, s), out.at[:, pl.ds(mine * me, mine)], ex_own.at[which]
                )
                own.start()
                owns.append(own)
            to_rows(buf, out, which, e_dp, 1 if k == 0 else 0)
        return owns[0]

    own_a.wait()
    pieces_wait(ex_recv.at[0])
    own_c = columns_back(cols_a, send_c, rows_c, 2, TN)
    own_b.wait()
    pieces_wait(ex_recv.at[1])
    own_d = columns_back(cols_b, send_d, rows_d, 3, NN)

    scale = 1.0 / (traces * width)

    def second_grad(q, carry):
        a = jnp.concatenate([cols_a[t, q] for t in range(traces * width)], axis=1)
        b = jnp.concatenate([cols_b[t, q] for t in range(traces * width)], axis=1)
        gs[q] = (dot(a, b, NT) * scale).astype(BF)
        return carry

    lax.fori_loop(0, mine, second_grad, 0)

    def gs_to(other):
        return remote(
            gs.at[:, block(other), :], gs_hbm.at[pl.ds(mine * d, mine)], gs_send, gs_recv, other, s
        )

    gs_mine = pltpu.make_async_copy(gs.at[:, block(d), :], gs_hbm.at[pl.ds(mine * d, mine)], gs_own)
    gs_mine.start()
    for other in (far, cross, near):
        gs_to(other).start()

    own_c.wait()
    pieces_wait(ex_recv.at[2])
    unpack(rows_c)

    def near_copy(p):
        return remote(gf_near.at[p], gf_near_in.at[p], near_send.at[p], near_recv.at[p], near, s)

    def far_copy(p):
        return remote(gf_far.at[p], gf_far_in.at[p], far_send.at[p], far_recv.at[p], far, s)

    def rows_back(p, carry):
        r = jnp.concatenate([tmp[t, row(p), :] for t in range(traces)], axis=1).astype(BF)
        gf_tmp[...] = dot(r, both(val, p), NT)
        gf_own[p, 0] = gf_tmp[block(d), :]
        gf_own[p, 1] = gf_tmp[block(far), :]
        gf_near[p, 0] = gf_tmp[block(near), :].astype(BF)
        gf_near[p, 1] = gf_tmp[block(cross), :].astype(BF)
        near_copy(p).start()
        v = dot(first[p], r, TN).astype(BF)
        for t in range(traces):
            part[t, p] = dot(v[:, t * channels : (t + 1) * channels], wv[...], NT)
        return carry

    lax.fori_loop(0, rows, rows_back, 0)

    def reduce_near(p, carry):
        near_copy(p).wait_recv()
        gf_far[p] = (gf_own[p, 1] + gf_near_in[p, 1].astype(F32)).astype(BF)
        far_copy(p).start()
        return carry

    lax.fori_loop(0, rows, reduce_near, 0)

    def reduce_far(p, carry):
        far_copy(p).wait_recv()
        near_copy(p).wait_send()
        total = gf_own[p, 0] + gf_near_in[p, 0].astype(F32) + gf_far_in[p].astype(F32)
        gf_near[p, 0] = (total * scale).astype(BF)
        pltpu.make_async_copy(gf_near.at[p, 0], gf_hbm.at[p], out_sem.at[0]).start()
        return carry

    lax.fori_loop(0, rows, reduce_far, 0)

    own_d.wait()
    pieces_wait(ex_recv.at[3])
    unpack(rows_d)

    def finish(i, carry):
        t, p = i // rows, lax.rem(i, rows)
        c = tmp[t, row(p), :]
        x[t, p] = (c * act[t, p]).astype(BF)
        g = (c * slope[t, p]).astype(BF)
        cot[t, p] = (part[t, p] + dot(g, wg[...], NT)).astype(BF)
        pltpu.make_async_copy(x.at[t, p], mixed_hbm.at[t, p], out_sem.at[1]).start()
        pltpu.make_async_copy(cot.at[t, p], gin_hbm.at[t, p], out_sem.at[2]).start()
        return carry

    lax.fori_loop(0, traces * rows, finish, 0)

    first_far.wait_send()
    first_near.wait_send()
    first_pass.wait_send()
    pltpu.make_async_copy(half, half, s_send).wait()
    for which in range(4):
        pieces_wait(ex_send.at[which])

    def sent(p, carry):
        far_copy(p).wait_send()
        return carry

    lax.fori_loop(0, rows, sent, 0)
    gs_mine.wait()
    three = gs.at[:, pl.ds(0, share * (width - 1)), :]
    pltpu.make_async_copy(three, three, gs_send).wait()
    pltpu.make_async_copy(three, three, gs_recv).wait()
    pltpu.make_async_copy(gf_far, gf_hbm, out_sem.at[0]).wait()
    pltpu.make_async_copy(x, mixed_hbm, out_sem.at[1]).wait()
    pltpu.make_async_copy(cot, gin_hbm, out_sem.at[2]).wait()


def on_device(traces_in, w_value, w_gate, first_blocks, second_blocks, cotangent):
    width, length = lax.axis_size("dp"), lax.axis_size("seq")
    traces, rows, columns, channels = traces_in.shape
    mine, share = columns // (width * length), columns // width
    by_row = (traces, columns, rows, channels)
    by_column = (traces * width, mine, rows * length, channels)
    hbm = pl.BlockSpec(memory_space=pl.ANY)
    dma = pltpu.SemaphoreType.DMA
    V = pltpu.VMEM
    shape = traces_in.shape
    return pl.pallas_call(
        kernel,
        out_shape=[
            jax.ShapeDtypeStruct(shape, BF),
            jax.ShapeDtypeStruct(shape, BF),
            jax.ShapeDtypeStruct(first_blocks.shape, BF),
            jax.ShapeDtypeStruct(second_blocks.shape, BF),
        ],
        in_specs=[hbm] * 6,
        out_specs=[hbm] * 4,
        scratch_shapes=[
            V(shape, BF), V(w_value.shape, BF), V(w_gate.shape, BF), V(shape, BF), V(shape, BF),
            V(shape, F32), V(shape, F32), V(shape, F32),
            V((rows, columns, columns), BF), V((mine, columns, columns), BF),
            V((traces, columns * rows, channels), F32),
            V(by_row, BF), V(by_row, BF), V(by_column, BF), V(by_column, BF),
            V(by_column, BF), V(by_column, BF), V(by_row, BF), V(by_row, BF),
            V((columns, columns), F32), V((rows, 2, share, columns), F32),
            V((rows, 2, share, columns), BF), V((rows, 2, share, columns), BF),
            V((rows, share, columns), BF), V((rows, share, columns), BF),
            V((mine, columns, columns), BF),
            dma((6,)), dma((3,)), dma((3,)), dma, dma, dma((4,)), dma((4,)), dma((4,)),
            dma((rows,)), dma((rows,)), dma((rows,)), dma((rows,)), dma, dma, dma, dma((3,)),
        ],
        compiler_params=pltpu.CompilerParams(
            collective_id=1, has_side_effects=True, vmem_limit_bytes=60 << 20
        ),
    )(traces_in, w_value, w_gate, first_blocks, second_blocks, cotangent)


def solution(mesh):
    big, weight = P("dp", "seq", None, None), P("seq", "dp", None)
    return jax.shard_map(
        on_device,
        mesh=mesh,
        in_specs=(big, P(), P(), weight, weight, big),
        out_specs=(big, big, weight, weight),
        check_vma=False,
    )
```

time: 448 us -> 278 us (0.62)
  Pallas kernels: 0 us -> 270 us
  blocking collectives: 232 us -> 0 us
  waiting for transfers between devices: 125 us -> 0 us
  matrix products: 42.5 us -> 0 us
  local copies, waits for them, and re-layouts: 28.8 us -> 7.79 us
  between operations: 13.8 us -> 0.65 us
  other arithmetic: 4.8 us -> 0 us
    pallas_call x0 -> x1, Pallas kernels: none -> 270 us  [on_device(): pl.pallas_call(kernel, out_shape=[jax.ShapeDtypeStruct(shape, BF), jax.Sh...]
    all_to_all x4 -> x0, blocking collectives: 232 us -> none  [the longest x1 88.4 us: on_device(): lax.all_to_all(rowmix, 'seq', split_axis=2, concat_axis=1, tiled=True)]
    reduce_scatter x2 -> x0, waiting for transfers between devices: 70.8 us -> none  [the longest x1 49.5 us: on_device(): lax.psum_scatter(first_part.astype(jnp.bfloat16), 'dp', scatter_dimension...]
    all_gather x2 -> x0, waiting for transfers between devices: 52.5 us -> none  [the longest x1 52.5 us: on_device(): lax.all_gather(first_blocks, 'dp', axis=1, tiled=True)]
    dot_general x9 -> x0, matrix products: 42.5 us -> none  [the longest x1 8.26 us: on_device(): jnp.einsum('tpqd,cd->tpqc', d_gate, w_gate, preferred_element_type=jnp.fl...]
    convert_element_type x4 -> x0, local copies, waits for them, and re-layouts: 18.6 us -> none  [the longest x1 6.17 us: on_device(): rowmix = jnp.einsum('pij,tpjc->tpic', full_first, values, preferred_eleme...]
    convert_element_type x2 -> x0, other arithmetic: 4.8 us -> none  [the longest x1 2.4 us: on_device(): grad_second = (second_sum / trace_count).astype(jnp.bfloat16)]
  transfers between devices with their start and end apart: 4 -> 0, of which waited for: 3 -> 0; matrix products, arithmetic and copies ran while one was open for 10% -> 0% of each run, Pallas kernels for 0% -> 0%
where the time goes in v2:
time: 278 us
  Pallas kernels  270 us (97%)
  local copies, waits for them, and re-layouts  7.79 us (3%)
    pallas_call x1, Pallas kernels, on_device(): pl.pallas_call(kernel, out_shape=[jax.ShapeDtypeStruct(shape, BF), jax.Sh...  270 us
    unnamed x10, local copies, waits for them, and re-layouts  7.79 us

profile of v2, /device:TPU:1, one launch (start us, length us, event | category | flops | bytes accessed | tf_op | source)
XLA Modules:
  0.0 278.2 jit_solution(2460393832409700630)
XLA Ops:
  0.6 269.7 %shard_map.93 = (bf16[2,8,512,128]{3,2,1,0:T(8,128)(2,1)}, bf16[2,8,512,128]{3,2,1,0:T(8,128)(2,1)}, bf16[8,128,512]{2,1,0:T(8,128)(2,1)}, bf16[8,128,512]{2,1,0:T(8,128)(2,1)}) custom-call(bf16[2,8,512,128]{3,2,1,0:T(8,128)(2,1)} %x_hbm.1, bf16[128,128]{1,0:T(8,128)(2,1)} %wv_hbm.1, bf16[128,128]{1,0:T(8,128)(2,1)} %wg_hbm.1, ...), custom_call_target="tpu_custom_call" | custom-call | tf_op jit(solution)/shard_map/pallas_call | solution.py:350
  270.4 0.0 copy-start
  270.4 3.3 %copy.14 = bf16[2,8,512,128]{3,2,1,0:T(8,128)(2,1)} copy(bf16[2,8,512,128]{3,2,1,0:T(8,128)(2,1)} %get-tuple-element.8) | data formatting | bytes 4194304
  273.7 0.0 copy-done
  273.7 0.0 copy-start.2
  273.7 1.3 copy.15
  275.0 0.6 copy-done.2
  275.6 0.0 copy-start.1
  275.6 1.0 copy.16
  276.6 0.6 copy-done.1
  277.2 1.0 copy.17
Async XLA Ops:
  270.4 3.3 %copy-start = (bf16[2,8,512,128]{3,2,1,0:T(8,128)(2,1)S(1)}, bf16[2,8,512,128]{3,2,1,0:T(8,128)(2,1)}, u32[]{:S(2)}) copy-start(bf16[2,8,512,128]{3,2,1,0:T(8,128)(2,1)} %get-tuple-element.9) | copy-start | bytes 6291460
  273.7 2.0 copy-start.2
  275.6 1.6 copy-start.1

commit v3 on v2

--- a/solution.py
+++ b/solution.py
@@ -19,13 +19,14 @@
 
 def kernel(
     x_hbm, wv_hbm, wg_hbm, first_hbm, second_hbm, cot_hbm,
-    mixed_hbm, gin_hbm, gf_hbm, gs_hbm,
-    x, wv, wg, cot, val, act, slope, part, first, second, tmp,
+    mixed, gin, gf, gs_out,
+    wv, wg, val, act, slope, part, first, second, tmp,
     send_a, send_b, cols_a, cols_b, send_c, send_d, rows_c, rows_d,
     gf_tmp, gf_own, gf_near, gf_near_in, gf_far, gf_far_in, gs,
     in_sem, f_send, f_recv, s_send, s_recv, ex_send, ex_recv, ex_own,
-    near_send, near_recv, far_send, far_recv, gs_send, gs_recv, gs_own, out_sem,
+    near_send, near_recv, far_send, far_recv, gs_send, gs_recv, gs_own, group, ready,
 ):
+    x, cot = mixed, gin
     width, length = lax.axis_size("dp"), lax.axis_size("seq")
     n = width * length
     traces, rows, columns, channels = x.shape
@@ -55,15 +56,22 @@
 
     barrier = pltpu.get_barrier_semaphore()
 
-    def greet(k, carry):
-        e = lax.rem(me + k, n)
-        pl.semaphore_signal(
-            barrier, inc=1, device_id=(lax.rem(e, width), e // width), device_id_type=MESH
-        )
-        return carry
-
-    lax.fori_loop(1, n, greet, 0)
-    pl.semaphore_wait(barrier, n - 1)
+    def signal(sem, to_dp, to_seq):
+        pl.semaphore_signal(sem, inc=1, device_id=(to_dp, to_seq), device_id_type=MESH)
+
+    @pl.when(d != 0)
+    def _():
+        signal(barrier, 0, s)
+
+    @pl.when(d == 0)
+    def _():
+        pl.semaphore_wait(barrier, width - 1)
+        for other in range(1, width):
+            signal(group, other, s)
+
+    @pl.when(d != 0)
+    def _():
+        pl.semaphore_wait(group, 1)
 
     def remote(a, b, send, recv, to_dp, to_seq):
         return pltpu.make_async_remote_copy(
@@ -80,6 +88,23 @@
     )
     first_far.start()
     first_near.start()
+
+    def second_to(other):
+        return remote(
+            second_hbm.at[pl.ds(mine * other, mine)], second.at[:, block(d), :],
+            s_send, s_recv, other, s,
+        )
+
+    for other in (far, cross, near):
+        second_to(other).start()
+
+    @pl.when(d == 1)
+    def _():
+        def greet(k, carry):
+            signal(barrier, 1, lax.rem(s + k, length))
+            return carry
+
+        lax.fori_loop(1, length, greet, 0)
 
     def pieces_wait(sem):
         rest = send_a.at[:, pl.ds(0, columns - mine)]
@@ -161,19 +186,22 @@
         tmp[t, row(p), :] = c * a
         return carry
 
-    lax.fori_loop(0, traces * rows, gate, 0)
+    lax.fori_loop(0, rows, gate, 0)
+
+    @pl.when(d == 1)
+    def _():
+        pl.semaphore_wait(barrier, length - 1)
+        for other in (0, *range(2, width)):
+            signal(ready, other, s)
+
+    lax.fori_loop(rows, traces * rows, gate, 0)
     pack(send_a)
+
+    @pl.when(d != 1)
+    def _():
+        pl.semaphore_wait(ready, 1)
+
     own_a = to_columns(send_a, cols_a, 0)
-
-    def second_to(other):
-        return remote(
-            second_hbm.at[pl.ds(mine * other, mine)], second.at[:, block(d), :],
-            s_send, s_recv, other, s,
-        )
-
-    for other in (far, cross, near):
-        second_to(other).start()
-
     loads[3].wait()
 
     def value(i, carry):
@@ -249,10 +277,10 @@
 
     def gs_to(other):
         return remote(
-            gs.at[:, block(other), :], gs_hbm.at[pl.ds(mine * d, mine)], gs_send, gs_recv, other, s
+            gs.at[:, block(other), :], gs_out.at[pl.ds(mine * d, mine)], gs_send, gs_recv, other, s
         )
 
-    gs_mine = pltpu.make_async_copy(gs.at[:, block(d), :], gs_hbm.at[pl.ds(mine * d, mine)], gs_own)
+    gs_mine = pltpu.make_async_copy(gs.at[:, block(d), :], gs_out.at[pl.ds(mine * d, mine)], gs_own)
     gs_mine.start()
     for other in (far, cross, near):
         gs_to(other).start()
@@ -285,36 +313,38 @@
     def reduce_near(p, carry):
         near_copy(p).wait_recv()
         gf_far[p] = (gf_own[p, 1] + gf_near_in[p, 1].astype(F32)).astype(BF)
+        gf_own[p, 0] = gf_own[p, 0] + gf_near_in[p, 0].astype(F32)
+        return carry
+
+    lax.fori_loop(0, rows, reduce_near, 0)
+
+    def send_far(p, carry):
         far_copy(p).start()
         return carry
 
-    lax.fori_loop(0, rows, reduce_near, 0)
-
-    def reduce_far(p, carry):
-        far_copy(p).wait_recv()
-        near_copy(p).wait_send()
-        total = gf_own[p, 0] + gf_near_in[p, 0].astype(F32) + gf_far_in[p].astype(F32)
-        gf_near[p, 0] = (total * scale).astype(BF)
-        pltpu.make_async_copy(gf_near.at[p, 0], gf_hbm.at[p], out_sem.at[0]).start()
-        return carry
-
-    lax.fori_loop(0, rows, reduce_far, 0)
+    lax.fori_loop(0, rows // 2, send_far, 0)
 
     own_d.wait()
     pieces_wait(ex_recv.at[3])
+    lax.fori_loop(rows // 2, rows, send_far, 0)
     unpack(rows_d)
 
     def finish(i, carry):
         t, p = i // rows, lax.rem(i, rows)
         c = tmp[t, row(p), :]
-        x[t, p] = (c * act[t, p]).astype(BF)
+        mixed[t, p] = (c * act[t, p]).astype(BF)
         g = (c * slope[t, p]).astype(BF)
-        cot[t, p] = (part[t, p] + dot(g, wg[...], NT)).astype(BF)
-        pltpu.make_async_copy(x.at[t, p], mixed_hbm.at[t, p], out_sem.at[1]).start()
-        pltpu.make_async_copy(cot.at[t, p], gin_hbm.at[t, p], out_sem.at[2]).start()
+        gin[t, p] = (part[t, p] + dot(g, wg[...], NT)).astype(BF)
         return carry
 
     lax.fori_loop(0, traces * rows, finish, 0)
+
+    def reduce_far(p, carry):
+        far_copy(p).wait_recv()
+        gf[p] = ((gf_own[p, 0] + gf_far_in[p].astype(F32)) * scale).astype(BF)
+        return carry
+
+    lax.fori_loop(0, rows, reduce_far, 0)
 
     first_far.wait_send()
     first_near.wait_send()
@@ -325,6 +355,7 @@
 
     def sent(p, carry):
         far_copy(p).wait_send()
+        near_copy(p).wait_send()
         return carry
 
     lax.fori_loop(0, rows, sent, 0)
@@ -332,9 +363,18 @@
     three = gs.at[:, pl.ds(0, share * (width - 1)), :]
     pltpu.make_async_copy(three, three, gs_send).wait()
     pltpu.make_async_copy(three, three, gs_recv).wait()
-    pltpu.make_async_copy(gf_far, gf_hbm, out_sem.at[0]).wait()
-    pltpu.make_async_copy(x, mixed_hbm, out_sem.at[1]).wait()
-    pltpu.make_async_copy(cot, gin_hbm, out_sem.at[2]).wait()
+
+
+def write_kernel(*refs):
+    sem = refs[-1]
+    half = len(refs) // 2
+    copies = [
+        pltpu.make_async_copy(a, b, sem.at[i]) for i, (a, b) in enumerate(zip(refs[:half], refs[half:-1]))
+    ]
+    for copy in copies:
+        copy.start()
+    for copy in copies:
+        copy.wait()
 
 
 def on_device(traces_in, w_value, w_gate, first_blocks, second_blocks, cotangent):
@@ -347,18 +387,20 @@
     dma = pltpu.SemaphoreType.DMA
     V = pltpu.VMEM
     shape = traces_in.shape
-    return pl.pallas_call(
+    vmem = pl.BlockSpec(memory_space=pltpu.VMEM)
+    out_shape = [
+        jax.ShapeDtypeStruct(shape, BF),
+        jax.ShapeDtypeStruct(shape, BF),
+        jax.ShapeDtypeStruct(first_blocks.shape, BF),
+        jax.ShapeDtypeStruct(second_blocks.shape, BF),
+    ]
+    outs = pl.pallas_call(
         kernel,
-        out_shape=[
-            jax.ShapeDtypeStruct(shape, BF),
-            jax.ShapeDtypeStruct(shape, BF),
-            jax.ShapeDtypeStruct(first_blocks.shape, BF),
-            jax.ShapeDtypeStruct(second_blocks.shape, BF),
-        ],
+        out_shape=[pltpu.VMEM(o.shape, o.dtype) for o in out_shape],
         in_specs=[hbm] * 6,
-        out_specs=[hbm] * 4,
+        out_specs=[vmem] * 4,
         scratch_shapes=[
-            V(shape, BF), V(w_value.shape, BF), V(w_gate.shape, BF), V(shape, BF), V(shape, BF),
+            V(w_value.shape, BF), V(w_gate.shape, BF), V(shape, BF),
             V(shape, F32), V(shape, F32), V(shape, F32),
             V((rows, columns, columns), BF), V((mine, columns, columns), BF),
             V((traces, columns * rows, channels), F32),
@@ -369,12 +411,21 @@
             V((rows, share, columns), BF), V((rows, share, columns), BF),
             V((mine, columns, columns), BF),
             dma((6,)), dma((3,)), dma((3,)), dma, dma, dma((4,)), dma((4,)), dma((4,)),
-            dma((rows,)), dma((rows,)), dma((rows,)), dma((rows,)), dma, dma, dma, dma((3,)),
+            dma((rows,)), dma((rows,)), dma((rows,)), dma((rows,)), dma, dma, dma,
+            pltpu.SemaphoreType.REGULAR, pltpu.SemaphoreType.REGULAR,
         ],
         compiler_params=pltpu.CompilerParams(
-            collective_id=1, has_side_effects=True, vmem_limit_bytes=60 << 20
+            collective_id=1, has_side_effects=True, vmem_limit_bytes=52 << 20
         ),
     )(traces_in, w_value, w_gate, first_blocks, second_blocks, cotangent)
+    return pl.pallas_call(
+        write_kernel,
+        out_shape=out_shape,
+        in_specs=[vmem] * 4,
+        out_specs=[hbm] * 4,
+        scratch_shapes=[dma((4,))],
+        compiler_params=pltpu.CompilerParams(vmem_limit_bytes=8 << 20),
+    )(*[pltpu.with_memory_space_constraint(o, pltpu.VMEM) for o in outs])
 
 
 def solution(mesh):

time: 278 us -> 257 us (0.924)
  Pallas kernels: 270 us -> 256 us
  local copies, waits for them, and re-layouts: 7.79 us -> 0 us
    pallas_call x1 -> x2, Pallas kernels: 270 us -> 256 us  [the longest x1 254 us: on_device(): pl.pallas_call(kernel, out_shape=[pltpu.VMEM(o.shape, o.dtype) for o in o...]
    unnamed x10 -> x0, local copies, waits for them, and re-layouts: 7.79 us -> none
where the time goes in v3:
time: 257 us
  Pallas kernels  256 us (100%)
    pallas_call x1, Pallas kernels, on_device(): pl.pallas_call(kernel, out_shape=[pltpu.VMEM(o.shape, o.dtype) for o in o...  254 us

profile of v3, /device:TPU:1, one launch (start us, length us, event | category | flops | bytes accessed | tf_op | source)
XLA Modules:
  0.0 257.1 jit_solution(1456843456010181885)
XLA Ops:
  0.6 253.8 %shard_map.93 = (bf16[2,8,512,128]{3,2,1,0:T(8,128)(2,1)S(1)}, bf16[2,8,512,128]{3,2,1,0:T(8,128)(2,1)S(1)}, bf16[8,128,512]{2,1,0:T(8,128)(2,1)S(1)}, bf16[8,128,512]{2,1,0:T(8,128)(2,1)S(1)}) custom-call(bf16[2,8,512,128]{3,2,1,0:T(8,128)(2,1)} %x_hbm.1, bf16[128,128]{1,0:T(8,128)(2,1)} %wv_hbm.1, bf16[128,128]{1,0:T(8,128)(2,1)} %wg_hbm.1, ...), custom_call_target="tpu_custom_call" | custom-call | tf_op jit(solution)/shard_map/pallas_call | solution.py:397
  254.4 2.7 %shard_map.94 = (bf16[2,8,512,128]{3,2,1,0:T(8,128)(2,1)}, bf16[2,8,512,128]{3,2,1,0:T(8,128)(2,1)}, bf16[8,128,512]{2,1,0:T(8,128)(2,1)}, bf16[8,128,512]{2,1,0:T(8,128)(2,1)}) custom-call(bf16[2,8,512,128]{3,2,1,0:T(8,128)(2,1)S(1)} %get-tuple-element.8.refs_0_, bf16[2,8,512,128]{3,2,1,0:T(8,128)(2,1)S(1)} %get-tuple-element.9.refs_1_, ...), custom_call_target="tpu_custom_call" | custom-call | tf_op jit(solution)/shard_map/pallas_call | solution.py:421

commit v4 on v3

--- a/solution.py
+++ b/solution.py
@@ -51,25 +51,29 @@
             ]
         )
     ]
+    barrier = pltpu.get_barrier_semaphore()
+
+    def signal(sem, to_dp, to_seq):
+        pl.semaphore_signal(sem, inc=1, device_id=(to_dp, to_seq), device_id_type=MESH)
+
+    for other in (0, *range(2, width)):
+
+        @pl.when(d != other)
+        def _(other=other):
+            signal(barrier, other, s)
+
     for load in loads:
         load.start()
 
-    barrier = pltpu.get_barrier_semaphore()
-
-    def signal(sem, to_dp, to_seq):
-        pl.semaphore_signal(sem, inc=1, device_id=(to_dp, to_seq), device_id_type=MESH)
-
-    @pl.when(d != 0)
-    def _():
-        signal(barrier, 0, s)
+    @pl.when(d != 1)
+    def _():
+        pl.semaphore_wait(barrier, width - 1)
 
     @pl.when(d == 0)
     def _():
-        pl.semaphore_wait(barrier, width - 1)
-        for other in range(1, width):
-            signal(group, other, s)
-
-    @pl.when(d != 0)
+        signal(group, 1, s)
+
+    @pl.when(d == 1)
     def _():
         pl.semaphore_wait(group, 1)
 
@@ -339,13 +343,6 @@
 
     lax.fori_loop(0, traces * rows, finish, 0)
 
-    def reduce_far(p, carry):
-        far_copy(p).wait_recv()
-        gf[p] = ((gf_own[p, 0] + gf_far_in[p].astype(F32)) * scale).astype(BF)
-        return carry
-
-    lax.fori_loop(0, rows, reduce_far, 0)
-
     first_far.wait_send()
     first_near.wait_send()
     first_pass.wait_send()
@@ -353,24 +350,39 @@
     for which in range(4):
         pieces_wait(ex_send.at[which])
 
-    def sent(p, carry):
-        far_copy(p).wait_send()
-        near_copy(p).wait_send()
-        return carry
-
-    lax.fori_loop(0, rows, sent, 0)
     gs_mine.wait()
     three = gs.at[:, pl.ds(0, share * (width - 1)), :]
     pltpu.make_async_copy(three, three, gs_send).wait()
     pltpu.make_async_copy(three, three, gs_recv).wait()
 
+    def near_sent(p, carry):
+        near_copy(p).wait_send()
+        return carry
+
+    lax.fori_loop(0, rows, near_sent, 0)
+
+    def reduce_far(p, carry):
+        far_copy(p).wait_recv()
+        gf[p] = ((gf_own[p, 0] + gf_far_in[p].astype(F32)) * scale).astype(BF)
+        return carry
+
+    lax.fori_loop(0, rows, reduce_far, 0)
+
+    def sent(p, carry):
+        far_copy(p).wait_send()
+        return carry
+
+    lax.fori_loop(0, rows, sent, 0)
+
 
 def write_kernel(*refs):
     sem = refs[-1]
     half = len(refs) // 2
-    copies = [
-        pltpu.make_async_copy(a, b, sem.at[i]) for i, (a, b) in enumerate(zip(refs[:half], refs[half:-1]))
-    ]
+    copies = []
+    for a, b in zip(refs[:half], refs[half:-1]):
+        cut = a.shape[0] // 2
+        for part in (pl.ds(0, cut), pl.ds(cut, cut)):
+            copies.append(pltpu.make_async_copy(a.at[part], b.at[part], sem.at[len(copies)]))
     for copy in copies:
         copy.start()
     for copy in copies:
@@ -423,7 +435,7 @@
         out_shape=out_shape,
         in_specs=[vmem] * 4,
         out_specs=[hbm] * 4,
-        scratch_shapes=[dma((4,))],
+        scratch_shapes=[dma((8,))],
         compiler_params=pltpu.CompilerParams(vmem_limit_bytes=8 << 20),
     )(*[pltpu.with_memory_space_constraint(o, pltpu.VMEM) for o in outs])
 

time: 257 us -> 257 us (level)
  no operation moved by 1% of the time
where the time goes in v4:
time: 257 us
  Pallas kernels  256 us (100%)
    pallas_call x1, Pallas kernels, on_device(): pl.pallas_call(kernel, out_shape=[pltpu.VMEM(o.shape, o.dtype) for o in o...  254 us

profile of v4, /device:TPU:1, one launch (start us, length us, event | category | flops | bytes accessed | tf_op | source)
XLA Modules:
  0.0 256.9 jit_solution(12865938053925738526)
XLA Ops:
  0.6 253.6 %shard_map.93 = (bf16[2,8,512,128]{3,2,1,0:T(8,128)(2,1)S(1)}, bf16[2,8,512,128]{3,2,1,0:T(8,128)(2,1)S(1)}, bf16[8,128,512]{2,1,0:T(8,128)(2,1)S(1)}, bf16[8,128,512]{2,1,0:T(8,128)(2,1)S(1)}) custom-call(bf16[2,8,512,128]{3,2,1,0:T(8,128)(2,1)} %x_hbm.1, bf16[128,128]{1,0:T(8,128)(2,1)} %wv_hbm.1, bf16[128,128]{1,0:T(8,128)(2,1)} %wg_hbm.1, ...), custom_call_target="tpu_custom_call" | custom-call | tf_op jit(solution)/shard_map/pallas_call | solution.py:409
  254.2 2.7 %shard_map.94 = (bf16[2,8,512,128]{3,2,1,0:T(8,128)(2,1)}, bf16[2,8,512,128]{3,2,1,0:T(8,128)(2,1)}, bf16[8,128,512]{2,1,0:T(8,128)(2,1)}, bf16[8,128,512]{2,1,0:T(8,128)(2,1)}) custom-call(bf16[2,8,512,128]{3,2,1,0:T(8,128)(2,1)S(1)} %get-tuple-element.8.refs_0_, bf16[2,8,512,128]{3,2,1,0:T(8,128)(2,1)S(1)} %get-tuple-element.9.refs_1_, ...), custom_call_target="tpu_custom_call" | custom-call | tf_op jit(solution)/shard_map/pallas_call | solution.py:433

commit v5 on v3

--- a/solution.py
+++ b/solution.py
@@ -135,12 +135,12 @@
             pl.ds(traces * e_dp, traces), :, pl.ds(pl.multiple_of(rows * e_seq, rows), rows), :
         ]
 
-    def to_rows(buf, out, which, e_dp, first_k):
+    def to_rows(buf, out, which, came, e_dp, first_k):
         def send(k, carry):
             e_seq = lax.rem(s + k, length)
             remote(
                 source(buf, e_dp, e_seq), out.at[:, pl.ds(mine * me, mine)],
-                ex_send.at[which], ex_recv.at[which], e_dp, e_seq,
+                ex_send.at[which], ex_recv.at[came], e_dp, e_seq,
             ).start()
             return carry
 
@@ -234,7 +234,7 @@
     half = second.at[:, pl.ds(0, share * (width - 1)), :]
     pltpu.make_async_copy(half, half, s_recv).wait()
 
-    def columns_back(cols, buf, out, which, dims):
+    def columns_back(cols, buf, out, which, dims, apart):
         owns = []
         for k in range(width):
             e_dp = lax.rem(d + k, width)
@@ -255,15 +255,16 @@
                 )
                 own.start()
                 owns.append(own)
-            to_rows(buf, out, which, e_dp, 1 if k == 0 else 0)
+            came = which + k if apart else which
+            to_rows(buf, out, which, came, e_dp, 1 if k == 0 else 0)
         return owns[0]
 
     own_a.wait()
     pieces_wait(ex_recv.at[0])
-    own_c = columns_back(cols_a, send_c, rows_c, 2, TN)
+    own_c = columns_back(cols_a, send_c, rows_c, 2, TN, False)
     own_b.wait()
     pieces_wait(ex_recv.at[1])
-    own_d = columns_back(cols_b, send_d, rows_d, 3, NN)
+    own_d = columns_back(cols_b, send_d, rows_d, 3, NN, True)
 
     scale = 1.0 / (traces * width)
 
@@ -325,8 +326,15 @@
     lax.fori_loop(0, rows // 2, send_far, 0)
 
     own_d.wait()
-    pieces_wait(ex_recv.at[3])
+
+    def portion_wait(k):
+        some = send_a.at[:, pl.ds(0, mine * (length - (1 if k == 0 else 0)))]
+        pltpu.make_async_copy(some, some, ex_recv.at[3 + k]).wait()
+
+    for k in range(width - 1):
+        portion_wait(k)
     lax.fori_loop(rows // 2, rows, send_far, 0)
+    portion_wait(width - 1)
     unpack(rows_d)
 
     def finish(i, carry):
@@ -410,7 +418,7 @@
             V((rows, 2, share, columns), BF), V((rows, 2, share, columns), BF),
             V((rows, share, columns), BF), V((rows, share, columns), BF),
             V((mine, columns, columns), BF),
-            dma((6,)), dma((3,)), dma((3,)), dma, dma, dma((4,)), dma((4,)), dma((4,)),
+            dma((6,)), dma((3,)), dma((3,)), dma, dma, dma((4,)), dma((3 + width,)), dma((4,)),
             dma((rows,)), dma((rows,)), dma((rows,)), dma((rows,)), dma, dma, dma,
             pltpu.SemaphoreType.REGULAR, pltpu.SemaphoreType.REGULAR,
         ],

time: 257 us -> 257 us (level)
  no operation moved by 1% of the time
where the time goes in v5:
time: 257 us
  Pallas kernels  257 us (100%)
    pallas_call x1, Pallas kernels, on_device(): pl.pallas_call(kernel, out_shape=[pltpu.VMEM(o.shape, o.dtype) for o in o...  254 us

profile of v5, /device:TPU:1, one launch (start us, length us, event | category | flops | bytes accessed | tf_op | source)
XLA Modules:
  0.0 257.2 jit_solution(16329280661925817770)
XLA Ops:
  0.6 253.8 %shard_map.93 = (bf16[2,8,512,128]{3,2,1,0:T(8,128)(2,1)S(1)}, bf16[2,8,512,128]{3,2,1,0:T(8,128)(2,1)S(1)}, bf16[8,128,512]{2,1,0:T(8,128)(2,1)S(1)}, bf16[8,128,512]{2,1,0:T(8,128)(2,1)S(1)}) custom-call(bf16[2,8,512,128]{3,2,1,0:T(8,128)(2,1)} %x_hbm.1, bf16[128,128]{1,0:T(8,128)(2,1)} %wv_hbm.1, bf16[128,128]{1,0:T(8,128)(2,1)} %wg_hbm.1, ...), custom_call_target="tpu_custom_call" | custom-call | tf_op jit(solution)/shard_map/pallas_call | solution.py:405
  254.5 2.7 %shard_map.94 = (bf16[2,8,512,128]{3,2,1,0:T(8,128)(2,1)}, bf16[2,8,512,128]{3,2,1,0:T(8,128)(2,1)}, bf16[8,128,512]{2,1,0:T(8,128)(2,1)}, bf16[8,128,512]{2,1,0:T(8,128)(2,1)}) custom-call(bf16[2,8,512,128]{3,2,1,0:T(8,128)(2,1)S(1)} %get-tuple-element.8.refs_0_, bf16[2,8,512,128]{3,2,1,0:T(8,128)(2,1)S(1)} %get-tuple-element.9.refs_1_, ...), custom_call_target="tpu_custom_call" | custom-call | tf_op jit(solution)/shard_map/pallas_call | solution.py:429

commit v6 on v3

--- a/solution.py
+++ b/solution.py
@@ -282,8 +282,6 @@
 
     gs_mine = pltpu.make_async_copy(gs.at[:, block(d), :], gs_out.at[pl.ds(mine * d, mine)], gs_own)
     gs_mine.start()
-    for other in (far, cross, near):
-        gs_to(other).start()
 
     own_c.wait()
     pieces_wait(ex_recv.at[2])
@@ -322,11 +320,12 @@
         far_copy(p).start()
         return carry
 
-    lax.fori_loop(0, rows // 2, send_far, 0)
+    lax.fori_loop(0, rows, send_far, 0)
 
     own_d.wait()
     pieces_wait(ex_recv.at[3])
-    lax.fori_loop(rows // 2, rows, send_far, 0)
+    for other in (far, cross, near):
+        gs_to(other).start()
     unpack(rows_d)
 
     def finish(i, carry):

time: 257 us -> 257 us (level)
  no operation moved by 1% of the time
where the time goes in v6:
time: 257 us
  Pallas kernels  257 us (100%)
    pallas_call x1, Pallas kernels, on_device(): pl.pallas_call(kernel, out_shape=[pltpu.VMEM(o.shape, o.dtype) for o in o...  254 us

profile of v6, /device:TPU:1, one launch (start us, length us, event | category | flops | bytes accessed | tf_op | source)
XLA Modules:
  0.0 257.2 jit_solution(6331391765645924971)
XLA Ops:
  0.6 253.9 %shard_map.93 = (bf16[2,8,512,128]{3,2,1,0:T(8,128)(2,1)S(1)}, bf16[2,8,512,128]{3,2,1,0:T(8,128)(2,1)S(1)}, bf16[8,128,512]{2,1,0:T(8,128)(2,1)S(1)}, bf16[8,128,512]{2,1,0:T(8,128)(2,1)S(1)}) custom-call(bf16[2,8,512,128]{3,2,1,0:T(8,128)(2,1)} %x_hbm.1, bf16[128,128]{1,0:T(8,128)(2,1)} %wv_hbm.1, bf16[128,128]{1,0:T(8,128)(2,1)} %wg_hbm.1, ...), custom_call_target="tpu_custom_call" | custom-call | tf_op jit(solution)/shard_map/pallas_call | solution.py:396
  254.5 2.7 %shard_map.94 = (bf16[2,8,512,128]{3,2,1,0:T(8,128)(2,1)}, bf16[2,8,512,128]{3,2,1,0:T(8,128)(2,1)}, bf16[8,128,512]{2,1,0:T(8,128)(2,1)}, bf16[8,128,512]{2,1,0:T(8,128)(2,1)}) custom-call(bf16[2,8,512,128]{3,2,1,0:T(8,128)(2,1)S(1)} %get-tuple-element.8.refs_0_, bf16[2,8,512,128]{3,2,1,0:T(8,128)(2,1)S(1)} %get-tuple-element.9.refs_1_, ...), custom_call_target="tpu_custom_call" | custom-call | tf_op jit(solution)/shard_map/pallas_call | solution.py:420
